TPU v7x, 32 devices: a whole 2x2x4 slice. The times are simulated.
32 devices in a mesh: ctx: 8 (over z, y), wsh: 4 (over x, core).
Axes of the slice: x: 2, y: 2, z: 4, core: 2. Of those that a mesh axis runs over, the one named last changes fastest.
Arguments:
- tokens: bfloat16 [4, 1024, 2048], P('wsh', 'ctx'), may hold values from -6 to 6
- out_grad: bfloat16 [4, 1024, 2048], P('wsh', 'ctx'), may hold values from -6 to 6
- attn_weight: bfloat16 [4, 2048, 2048], P(None, None, 'wsh'), may hold values from -0.125 to 0.125
- mlp_weight: bfloat16 [3, 2048, 8192], P(None, None, 'wsh'), may hold values from -0.125 to 0.125
- norm_gains: bfloat16 [4, 2048], P(None, 'wsh'), may hold values from 0.25 to 1.75
- adapt_model: bfloat16 [11, 64, 2048], P(None, None, 'wsh'), may hold values from -0.125 to 0.125
- adapt_hidden: bfloat16 [3, 64, 8192], P(None, None, 'wsh'), may hold values from -0.0625 to 0.0625
- lengths: int32 [4], replicated, may hold values from 512 to 1024, as said below
- adapter_pick: int32 [4], replicated, may hold values from 0 to 3
- block_order: int32 [4, 16], P('wsh'), may hold values from 0 to 15, as said below
Outputs:
- layer_out: bfloat16 [4, 1024, 2048], P('wsh', 'ctx')
- input_grad: float32 [4, 1024, 2048], P('wsh', 'ctx')
- adapt_model_grad: float32 [11, 64, 2048], P(None, None, 'wsh')
- adapt_hidden_grad: float32 [3, 64, 8192], P(None, None, 'wsh')
Inputs may be any that keep to these rules, and one draw needn't show every extreme that they name: `lengths`: some sequence has exactly 1024 valid tokens. Each row of block_order is a permutation of the 16 blocks; the two blocks stored on one index of ctx are p and 15 - p for some p, in either order.
All inputs are finite; a program needn't handle non-finite values.
Results may differ from a plain program's by a relative error of at most 0.017.
Values may be sent and summed in bfloat16 or wider, within the bound.
No kernel may reach another device: no remote copies, remote signals or barrier semaphores. Data moves between devices by JAX's collectives and lax.ppermute only.
A program may use at most 512 MiB of HBM per device.

v0:
```python
import math
import jax
import jax.numpy as jnp
from jax import lax
from jax.sharding import PartitionSpec as P

HEADS = 16
HEAD_DIM = 128
RANK = 16
ADAPTERS = 4
NORM_EPS = 1e-06
ADAPTER_SCALE = 4.0
ROPE_BASE = 500000.0
F32 = jnp.float32
BF16 = jnp.bfloat16
CORE_SWAP = ((0, 1), (1, 0), (2, 3), (3, 2))
CHIP_SWAP = ((0, 2), (2, 0), (1, 3), (3, 1))


def dot(left, right, dims):
    return lax.dot_general(left, right, (dims, ((), ())), preferred_element_type=F32)


def mm(left, right):
    return dot(left, right, ((1,), (0,)))


def mm_t(left, right):
    return dot(left, right, ((1,), (1,)))


def tmm(left, right):
    return dot(left, right, ((0,), (0,)))


def swap_core(values):
    return lax.ppermute(values, "wsh", CORE_SWAP)


def swap_chip(values):
    return lax.ppermute(values, "wsh", CHIP_SWAP)


def sum_wsh(values):
    values = values + swap_core(values)
    return values + swap_chip(values)


def gather_wsh(block, axis, me):
    far = swap_chip(block)
    near = swap_core(block)
    far_near = swap_core(far)
    extent = block.shape[axis]
    shape = list(block.shape)
    shape[axis] = 4 * extent
    whole = jnp.zeros(shape, block.dtype)
    for flip, piece in ((0, block), (1, near), (2, far), (3, far_near)):
        start = [0] * block.ndim
        start[axis] = (me ^ flip) * extent
        whole = lax.dynamic_update_slice(whole, piece, start)
    return whole


def scatter_wsh(partial, axis, me):
    extent = partial.shape[axis] // 4

    def piece(flip):
        return lax.dynamic_slice_in_dim(partial, (me ^ flip) * extent, extent, axis)

    far = piece(2).astype(F32) + swap_core(piece(3)).astype(F32)
    far = swap_chip(far.astype(BF16))
    near = piece(0).astype(F32) + swap_core(piece(1)).astype(F32)
    return near + far.astype(F32)


def rotate(values, cosine, sine_part):
    half = HEAD_DIM // 2
    first, second = (values[..., :half], values[..., half:])
    return jnp.concatenate(
        [first * cosine - second * sine_part, second * cosine + first * sine_part], axis=-1
    )


def per_device(
    tokens,
    out_grad,
    attn_weight,
    mlp_weight,
    norm_gains,
    adapt_model,
    adapt_hidden,
    lengths,
    adapter_pick,
    block_order,
):
    own_rows = tokens[0]
    rows, model_dim = own_rows.shape
    block_rows = rows // 2
    ctx_size = lax.axis_size("ctx")
    seqs = lax.axis_size("wsh")
    width = model_dim // seqs
    local_heads = width // HEAD_DIM
    me = lax.axis_index("wsh")
    ctx_index = lax.axis_index("ctx")
    pairs = seqs * local_heads
    members = math.gcd(ctx_size, pairs)
    groups = ctx_size // members
    per_member = pairs // members
    splits = local_heads // per_member
    group_rows = members * rows
    member = ctx_index % members
    group = ctx_index // members
    ctx_groups = [[g * members + i for i in range(members)] for g in range(groups)]
    key_groups = [[g * members + i for g in range(groups)] for i in range(members)]
    score_scale = HEAD_DIM ** (-0.5)
    all_rows = seqs * rows

    def columns(matrix):
        return lax.dynamic_slice_in_dim(matrix, me * width, width, 1)

    orders = gather_wsh(block_order, 0, me)
    positions = (orders[:, :, None] * block_rows + jnp.arange(block_rows)[None, None, :]).reshape(
        seqs, -1
    )
    row_positions = lax.dynamic_slice_in_dim(positions, ctx_index * rows, rows, 1)
    own_positions = lax.dynamic_index_in_dim(row_positions, me, keepdims=False)
    own_length = lax.dynamic_index_in_dim(lengths, me, keepdims=False)
    valid_rows = (own_positions < own_length).astype(F32)[:, None]
    half_dim = HEAD_DIM // 2
    frequency = ROPE_BASE ** (-(jnp.arange(half_dim, dtype=F32) * 2.0) / HEAD_DIM)
    angles = row_positions.reshape(-1).astype(F32)[:, None] * frequency[None, :]
    cosine, sine_part = (jnp.cos(angles)[:, None, :], jnp.sin(angles)[:, None, :])
    picked = (jnp.arange(ADAPTERS * RANK)[None, :] // RANK == adapter_pick[:, None]).astype(F32)
    row_mask = jnp.broadcast_to(picked[:, None, :], (seqs, rows, ADAPTERS * RANK)).reshape(
        all_rows, -1
    )

    def low(product):
        return (product * row_mask).astype(BF16)

    def low_sum(partial):
        narrow = (partial * row_mask).reshape(all_rows, ADAPTERS, RANK).sum(1)
        total = jnp.tile(sum_wsh(narrow), (1, ADAPTERS))
        return (total * row_mask).astype(BF16)

    gains = norm_gains.astype(F32)
    last_gain = gather_wsh(norm_gains[3:4], 1, me).astype(F32)
    hidden = gather_wsh(own_rows, 0, me)
    rows_a = gather_wsh(jnp.concatenate([adapt_model[:6], adapt_model[10:11]], 0), 2, me)
    low_in = [low(mm_t(hidden, rows_a[k])) for k in range(3)]
    proj = [
        mm(hidden, attn_weight[k]) + ADAPTER_SCALE * mm(low_in[k], adapt_model[6 + k])
        for k in range(3)
    ]
    squares = jnp.stack([jnp.sum(proj[0] * proj[0], -1), jnp.sum(proj[1] * proj[1], -1)])
    scales = lax.rsqrt(sum_wsh(squares) / model_dim + NORM_EPS)[:, :, None]

    def heads(values):
        return values.reshape(all_rows, local_heads, HEAD_DIM)

    turned = [
        rotate(heads(proj[k] * scales[k] * gains[k]), cosine, sine_part).astype(BF16)
        for k in range(2)
    ]
    packed = jnp.stack([turned[0], turned[1], heads(proj[2].astype(BF16))])

    def to_heads(values):
        count = values.shape[0]
        shaped = values.reshape(count, seqs, rows, splits, per_member * HEAD_DIM)
        shaped = shaped.transpose(1, 3, 0, 2, 4).reshape(
            members, count, rows, per_member * HEAD_DIM
        )
        moved = lax.all_to_all(shaped, "ctx", 0, 0, tiled=True, axis_index_groups=ctx_groups)
        moved = moved.transpose(1, 0, 2, 3).reshape(count, group_rows, per_member, HEAD_DIM)
        return moved.transpose(0, 2, 1, 3)

    def to_rows(values):
        count = values.shape[0]
        shaped = values.transpose(0, 2, 1, 3).reshape(count, members, rows, per_member * HEAD_DIM)
        moved = lax.all_to_all(
            shaped.transpose(1, 0, 2, 3), "ctx", 0, 0, tiled=True, axis_index_groups=ctx_groups
        )
        moved = moved.reshape(seqs, splits, count, rows, per_member * HEAD_DIM)
        return moved.transpose(2, 0, 3, 1, 4).reshape(count, all_rows, width)

    queries, keys, values = to_heads(packed)
    if groups > 1:
        keys, values = (
            lax.all_gather(part, "ctx", axis=1, tiled=True, axis_index_groups=key_groups)
            for part in (keys, values)
        )
    seq_here = member * per_member // local_heads
    key_positions = lax.dynamic_index_in_dim(positions, seq_here, keepdims=False)
    query_positions = lax.dynamic_slice_in_dim(key_positions, group * group_rows, group_rows)
    length_here = lax.dynamic_index_in_dim(lengths, seq_here, keepdims=False)
    allowed = (key_positions[None, :] <= query_positions[:, None]) & (
        key_positions[None, :] < length_here
    )

    def batched(left, right, lc, rc):
        return lax.dot_general(
            left, right, (((lc,), (rc,)), ((0,), (0,))), preferred_element_type=F32
        )

    scores = jnp.where(allowed[None], batched(queries, keys, 2, 2) * score_scale, -jnp.inf)
    row_max = jnp.max(scores, axis=-1, keepdims=True)
    log_total = row_max + jnp.log(jnp.sum(jnp.exp(scores - row_max), axis=-1, keepdims=True))
    weights = jnp.exp(scores - log_total).astype(BF16)
    attended = batched(weights, values, 2, 1).astype(BF16)
    attended = to_rows(attended[None])[0]
    attended_full = gather_wsh(attended, 1, me)
    low_out = low(mm_t(attended_full, rows_a[3]))
    branch = mm(attended_full, attn_weight[3]) + ADAPTER_SCALE * mm(low_out, adapt_model[9])
    branch_scale = lax.rsqrt(
        sum_wsh(jnp.sum(branch * branch, -1, keepdims=True)) / model_dim + NORM_EPS
    )
    mid = columns(hidden).astype(F32) + branch * branch_scale * gains[2]
    mid_low = mid.astype(BF16)
    mid_full = gather_wsh(mid_low, 1, me)
    low_gate = low(mm_t(mid_full, rows_a[4]))
    low_up = low(mm_t(mid_full, rows_a[5]))
    gate = mm(mid_full, mlp_weight[0]) + ADAPTER_SCALE * mm(low_gate, adapt_hidden[0])
    up = mm(mid_full, mlp_weight[1]) + ADAPTER_SCALE * mm(low_up, adapt_hidden[1])
    sigmoid_gate = jax.nn.sigmoid(gate)
    silu_gate = gate * sigmoid_gate
    product = (silu_gate * up).astype(BF16)
    low_down_part = mm_t(product, adapt_hidden[2])
    down_part = mm_t(product, mlp_weight[2]) + ADAPTER_SCALE * mm(low(low_down_part), rows_a[6])
    down = scatter_wsh(down_part.astype(BF16), 0, me)
    low_down = low_sum(low_down_part)
    down_scale = lax.rsqrt(jnp.mean(down * down, axis=-1, keepdims=True) + NORM_EPS)
    mid_rows = lax.dynamic_slice_in_dim(mid_full, me * rows, rows, 0).astype(F32)
    result = mid_rows + down * down_scale * last_gain
    upstream = out_grad[0].astype(F32) * valid_rows
    scaled = upstream * last_gain
    grad_down = (
        down_scale * scaled - down * down_scale**3 * jnp.mean(scaled * down, axis=-1, keepdims=True)
    ).astype(BF16)
    grad_down = gather_wsh(grad_down, 0, me)
    grad_low_down = low(ADAPTER_SCALE * mm_t(grad_down, rows_a[6]))
    grad_product = mm(grad_down, mlp_weight[2]) + mm(grad_low_down, adapt_hidden[2])
    grad_gate = (grad_product * up * sigmoid_gate * (1.0 + gate * (1.0 - sigmoid_gate))).astype(
        BF16
    )
    grad_up = (grad_product * silu_gate).astype(BF16)
    low_gate_part = ADAPTER_SCALE * mm_t(grad_gate, adapt_hidden[0])
    low_up_part = ADAPTER_SCALE * mm_t(grad_up, adapt_hidden[1])
    own_block = (jnp.arange(seqs) == me).astype(F32)[:, None, None]
    mid_part = (
        mm_t(grad_gate, mlp_weight[0])
        + mm_t(grad_up, mlp_weight[1])
        + mm(low(low_gate_part), rows_a[4])
        + mm(low(low_up_part), rows_a[5])
        + (own_block * upstream[None]).reshape(all_rows, model_dim)
    )
    grad_mid = scatter_wsh(mid_part.astype(BF16), 1, me)
    grad_low_gate = low_sum(low_gate_part)
    grad_low_up = low_sum(low_up_part)
    hidden_grads = jnp.stack(
        [
            ADAPTER_SCALE * tmm(low_gate, grad_gate),
            ADAPTER_SCALE * tmm(low_up, grad_up),
            tmm(grad_low_down, product),
        ]
    )
    grad_a_gate = tmm(grad_low_gate, mid_low)
    grad_a_up = tmm(grad_low_up, mid_low)
    grad_b_down = ADAPTER_SCALE * tmm(low_down, columns(grad_down))
    scaled = grad_mid * gains[2]
    mean = sum_wsh(jnp.sum(scaled * branch, axis=-1, keepdims=True)) / model_dim
    grad_branch = (branch_scale * scaled - branch * branch_scale**3 * mean).astype(BF16)
    low_out_part = ADAPTER_SCALE * mm_t(grad_branch, adapt_model[9])
    attended_part = mm_t(grad_branch, attn_weight[3]) + mm(low(low_out_part), rows_a[3])
    grad_attended = scatter_wsh(attended_part.astype(BF16), 1, me).astype(BF16)
    grad_low_out = low_sum(low_out_part)
    grad_b_out = ADAPTER_SCALE * tmm(low_out, grad_branch)
    grad_a_out = tmm(grad_low_out, attended)
    grad_heads = to_heads(grad_attended[None])[0]
    scores = jnp.where(allowed[None], batched(queries, keys, 2, 2) * score_scale, -jnp.inf)
    weights_full = jnp.exp(scores - log_total)
    grad_probs = batched(grad_heads, values, 2, 2)
    delta = jnp.sum(weights_full * grad_probs, axis=-1, keepdims=True)
    grad_scores = (weights_full * (grad_probs - delta)).astype(BF16)
    grad_queries = batched(grad_scores, keys, 2, 1) * score_scale
    grad_keys = batched(grad_scores, queries, 1, 1) * score_scale
    grad_values = batched(weights_full.astype(BF16), grad_heads, 1, 1)
    if groups > 1:
        grad_keys, grad_values = (
            lax.psum_scatter(
                part, "ctx", scatter_dimension=1, tiled=True, axis_index_groups=key_groups
            )
            for part in (grad_keys, grad_values)
        )
    grads = to_rows(jnp.stack([grad_queries, grad_keys, grad_values]).astype(BF16))
    turned = [
        rotate(heads(grads[k].astype(F32)), cosine, -sine_part).reshape(all_rows, width) * gains[k]
        for k in range(2)
    ]
    sums = jnp.stack([jnp.sum(turned[k] * proj[k], -1) for k in range(2)])
    means = (sum_wsh(sums) / model_dim)[:, :, None]
    grad_proj = [
        (scales[k] * turned[k] - proj[k] * scales[k] ** 3 * means[k]).astype(BF16) for k in range(2)
    ] + [grads[2]]
    low_parts = [ADAPTER_SCALE * mm_t(grad_proj[k], adapt_model[6 + k]) for k in range(3)]
    own_column = (jnp.arange(seqs) == me).astype(F32)[None, :, None]
    input_part = (
        mm_t(grad_proj[0], attn_weight[0])
        + mm_t(grad_proj[1], attn_weight[1])
        + mm_t(grad_proj[2], attn_weight[2])
        + mm(low(low_parts[0]), rows_a[0])
        + mm(low(low_parts[1]), rows_a[1])
        + mm(low(low_parts[2]), rows_a[2])
        + (own_column * grad_mid[:, None, :]).reshape(all_rows, model_dim)
    )
    grad_inputs = scatter_wsh(input_part.astype(BF16), 0, me)
    own_hidden = columns(hidden)
    grad_a_in = [tmm(low_sum(low_parts[k]), own_hidden) for k in range(3)]
    grad_b_in = [ADAPTER_SCALE * tmm(low_in[k], grad_proj[k]) for k in range(3)]
    model_grads = jnp.stack(
        grad_a_in + [grad_a_out, grad_a_gate, grad_a_up] + grad_b_in + [grad_b_out, grad_b_down]
    )
    model_grads = lax.psum(model_grads, "ctx")
    hidden_grads = lax.psum(hidden_grads, "ctx")
    return (result.astype(BF16)[None], grad_inputs[None], model_grads, hidden_grads)


def solution(mesh):
    in_specs = (
        P("wsh", "ctx", None),
        P("wsh", "ctx", None),
        P(None, None, "wsh"),
        P(None, None, "wsh"),
        P(None, "wsh"),
        P(None, None, "wsh"),
        P(None, None, "wsh"),
        P(),
        P(),
        P("wsh", None),
    )
    out_specs = (
        P("wsh", "ctx", None),
        P("wsh", "ctx", None),
        P(None, None, "wsh"),
        P(None, None, "wsh"),
    )
    return jax.shard_map(
        per_device, mesh=mesh, in_specs=in_specs, out_specs=out_specs, check_vma=False
    )
```

profile of v0, /device:TPU:0, one launch (start us, length us, event | category | flops | bytes accessed | tf_op | source)
XLA Modules:
  0.0 655.7 jit_solution(950616927271443762)
XLA Ops:
  7.2 3.0 collective-permute-start.4
  20.7 15.3 %collective-permute-done.7 = bf16[7,64,512]{2,1,0:T(8,128)(2,1)} collective-permute-done((bf16[7,64,512]{2,1,0:T(8,128)(2,1)}, bf16[7,64,512]{2,1,0:T(8,128)(2,1)}, u32[]{:S(2)}, u32[]{:S(2)}) %collective-permute-start.7) | collective-permute-done | bytes 458784 | tf_op jit(solution)/shard_map/ppermute | solution.py:41
  64.8 3.7 maximum_bitcast_fusion
  68.4 3.7 copy.160
  72.2 6.4 all-to-all-start
  81.7 34.0 %all-to-all-done = bf16[8,3,128,256]{3,2,1,0:T(8,128)(2,1)} async-done(((bf16[8,3,128,256]{3,2,1,0:T(8,128)(2,1)}), bf16[8,3,128,256]{3,2,1,0:T(8,128)(2,1)}, u32[]{:S(2)}, u32[]{:S(2)}) %all-to-all-start) | async-done | bytes 1572896 | tf_op jit(solution)/shard_map/all_to_all | solution.py:173
  115.7 2.8 copy.161
  118.4 3.7 reshape.481
  122.1 2.6 copy.162
  124.7 3.0 fusion.18
  131.0 4.8 fusion.75
  139.1 18.4 %all_to_all.20 = bf16[8,1,128,256]{2,3,1,0:T(8,128)(2,1)} all-to-all(bf16[8,1,128,256]{2,3,1,0:T(8,128)(2,1)S(1)} %copy.165), channel_id=1, replica_groups={{0,4,8,12,16,20,24,28},{1,5,9,13,17,21,25,29},{2,6,10,14,18,22,26,30},{..., dimensions={0} | all-to-all | bytes 1048576 | tf_op jit(solution)/shard_map/all_to_all | solution.py:180
  164.5 11.0 %collective-permute-done.12 = bf16[512,512]{0,1:T(8,128)(2,1)S(1)} collective-permute-done((bf16[512,512]{0,1:T(8,128)(2,1)S(1)}, bf16[512,512]{0,1:T(8,128)(2,1)S(1)}, u32[]{:S(2)}, u32[]{:S(2)}) %collective-permute-start.12) | collective-permute-done | bytes 524320 | tf_op jit(solution)/shard_map/ppermute | solution.py:41
  179.2 2.9 multiply_reduce_fusion.5
  189.8 11.3 %collective-permute-done.17 = bf16[512,512]{0,1:T(8,128)(2,1)S(1)} collective-permute-done((bf16[512,512]{0,1:T(8,128)(2,1)S(1)}, bf16[512,512]{0,1:T(8,128)(2,1)S(1)}, u32[]{:S(2)}, u32[]{:S(2)}) %collective-permute-start.17) | collective-permute-done | bytes 524320 | tf_op jit(solution)/shard_map/ppermute | solution.py:41
  207.7 11.6 %multiply_add_fusion.1 = f32[512,2048]{0,1:T(8,128)} fusion(f32[512,2048]{0,1:T(8,128)S(1)} %fusion.137, bf16[512,2048]{0,1:T(8,128)(2,1)S(1)} %constant_dynamic-update-slice_fusion.4, bf16[3,2048,2048]{2,1,0:T(8,128)(2,1)} %param.13), kind=kOutput, calls=%fused_computation.37 | convolution fusion | flops 4297064448 | bytes 18874368 | tf_op jit(solution)/shard_map/dot_general | solution.py:21
  219.3 13.1 %multiply_convert_fusion.3 = (bf16[512,2048]{0,1:T(8,128)(2,1)S(1)}, f32[512,2048]{0,1:T(8,128)}) fusion(f32[512,2048]{0,1:T(8,128)} %multiply_add_fusion.1, f32[512,2048]{0,1:T(8,128)S(1)} %fusion.134, bf16[512,2048]{0,1:T(8,128)(2,1)S(1)} %constant_dynamic-update-slice_fusion.4, bf16[3,2048,2048]{2,1,0:T(8,128)(2,1)} %param.13), kind=kOutput, calls=%fused_computation.33 | convolution fusion | flops 4303355904 | bytes 25165824 | tf_op jit(solution)/shard_map/dot_general | solution.py:21
  232.9 7.1 %fusion.2 = f32[512,2048]{0,1:T(8,128)S(1)} fusion(bf16[512,2048]{0,1:T(8,128)(2,1)S(1)} %get-tuple-element.95, bf16[3,2048,2048]{2,1,0:T(8,128)(2,1)} %param.13), kind=kOutput, calls=%fused_computation.2 | convolution fusion | flops 4294967296 | bytes 14680064 | tf_op jit(solution)/shard_map/dot_general | solution.py:21
  250.0 10.0 %collective-permute-done.23 = bf16[1,512]{1,0:T(2,128)(2,1)S(1)} collective-permute-done((bf16[1,512]{1,0:T(2,128)(2,1)S(1)}, bf16[1,512]{1,0:T(2,128)(2,1)S(1)}, u32[]{:S(2)}, u32[]{:S(2)}) %collective-permute-start.23) | collective-permute-done | bytes 1056 | tf_op jit(solution)/shard_map/ppermute | solution.py:41
  268.0 12.4 %collective-permute-done.26 = bf16[128,2048]{0,1:T(8,128)(2,1)S(1)} collective-permute-done((bf16[128,2048]{0,1:T(8,128)(2,1)S(1)}, bf16[128,2048]{0,1:T(8,128)(2,1)S(1)}, u32[]{:S(2)}, u32[]{:S(2)}) %collective-permute-start.26) | collective-permute-done | bytes 524320 | tf_op jit(solution)/shard_map/ppermute | solution.py:41
  284.9 10.0 %multiply_convert_fusion.1 = (bf16[512,2048]{0,1:T(8,128)(2,1)S(1)}, bf16[512,2048]{0,1:T(8,128)(2,1)S(1)}) fusion(f32[512,2048]{0,1:T(8,128)} %multiply_add_fusion.1, f32[512,2048]{0,1:T(8,128)} %get-tuple-element.96, f32[512,2048]{0,1:T(8,128)S(1)} %fusion.130, bf16[512,2048]{0,1:T(8,128)(2,1)S(1)} %constant_dynamic-update-slice_fusion, ...), kind=kOutput, calls=%fused_computation.30 | convolution fusion | flops 4309647360 | bytes 27262976 | tf_op jit(solution)/shard_map/dot_general | solution.py:21
  295.4 7.9 %fusion.8 = f32[512,2048]{0,1:T(8,128)S(1)} fusion(bf16[512,2048]{0,1:T(8,128)(2,1)S(1)} %get-tuple-element.39, bf16[3,2048,2048]{2,1,0:T(8,128)(2,1)} %param.13), kind=kOutput, calls=%fused_computation.8 | convolution fusion | flops 4294967296 | bytes 14680064 | tf_op jit(solution)/shard_map/dot_general | solution.py:21
  303.8 6.9 %fusion.4 = f32[512,2048]{0,1:T(8,128)S(1)} fusion(bf16[512,2048]{0,1:T(8,128)(2,1)S(1)} %get-tuple-element.38, bf16[3,2048,2048]{2,1,0:T(8,128)(2,1)} %param.13), kind=kOutput, calls=%fused_computation.4 | convolution fusion | flops 4294967296 | bytes 14680064 | tf_op jit(solution)/shard_map/dot_general | solution.py:21
  319.4 12.4 %collective-permute-done.30 = bf16[512,512]{0,1:T(8,128)(2,1)S(1)} collective-permute-done((bf16[512,512]{0,1:T(8,128)(2,1)S(1)}, bf16[512,512]{0,1:T(8,128)(2,1)S(1)}, u32[]{:S(2)}, u32[]{:S(2)}) %collective-permute-start.30) | collective-permute-done | bytes 524320 | tf_op jit(solution)/shard_map/ppermute | solution.py:41
  337.5 2.9 fusion.32
  346.0 12.4 %collective-permute-done.35 = bf16[512,512]{1,0:T(8,128)(2,1)S(1)} collective-permute-done((bf16[512,512]{1,0:T(8,128)(2,1)S(1)}, bf16[512,512]{1,0:T(8,128)(2,1)S(1)}, u32[]{:S(2)}, u32[]{:S(2)}) %collective-permute-start.35) | collective-permute-done | bytes 524320 | tf_op jit(solution)/shard_map/ppermute | solution.py:41
  362.5 18.6 %all_to_all.21 = bf16[8,1,128,256]{3,2,1,0:T(8,128)(2,1)} all-to-all(bf16[8,1,128,256]{3,2,1,0:T(8,128)(2,1)S(1)} %bitcast.544), channel_id=1, replica_groups={{0,4,8,12,16,20,24,28},{1,5,9,13,17,21,25,29},{2,6,10,14,18,22,26,30},{..., dimensions={0} | all-to-all | bytes 1048576 | tf_op jit(solution)/shard_map/all_to_all | solution.py:173
  383.1 5.5 fusion.76
  388.6 5.5 multiply_reduce_fusion
  394.1 2.7 multiply_convert_fusion
  401.2 2.6 copy.186
  407.2 4.5 all-to-all-start.3
  419.7 3.2 convolution_bitcast_fusion
  438.5 4.0 copy.219
  443.1 4.7 all-to-all-done.3
  447.8 2.6 copy.188
  450.4 2.9 fusion.192
  456.5 2.6 reshape.499
  461.7 2.6 reshape.498
  470.0 5.0 fusion.36
  481.6 5.1 fusion.40
  488.7 4.9 fusion.44
  496.2 3.8 fusion.139
  505.3 3.7 fusion.140
  520.6 10.5 %add_convert_fusion = bf16[512,2048]{1,0:T(8,128)(2,1)S(1)} fusion(f32[512,2048]{1,0:T(8,128)} %bitcast.518, f32[512,2048]{1,0:T(8,128)} %fusion.140, f32[512,2048]{1,0:T(8,128)} %fusion.139, f32[512,2048]{1,0:T(8,128)} %fusion.36, f32[512,2048]{1,0:T(8,128)} %fusion.44, f32[512,2048]{1,0:T(8,128)} %fusion.40, f32[2048]{0:T(1024)S(1)} %bitcast.557, ...), kind=kOutput, calls=%fused_computation.28 | convolution fusion | flops 142639104 | bytes 27664384 | tf_op jit(solution)/shard_map/dot_general | solution.py:21
  537.7 10.7 %collective-permute-done.40 = bf16[128,2048]{1,0:T(8,128)(2,1)} collective-permute-done((bf16[128,2048]{1,0:T(8,128)(2,1)S(1)}, bf16[128,2048]{1,0:T(8,128)(2,1)}, u32[]{:S(2)}, u32[]{:S(2)}) %collective-permute-start.40) | collective-permute-done | bytes 524320 | tf_op jit(solution)/shard_map/ppermute | solution.py:41
  551.0 93.8 %all-reduce.3.cloned.1.call-done = (f32[11,64,512]{2,1,0:T(8,128)}, f32[3,64,2048]{2,1,0:T(8,128)}) async-done(((f32[11,64,512]{2,1,0:T(8,128)}, f32[3,64,2048]{2,1,0:T(8,128)}), (f32[11,64,512]{2,1,0:T(8,128)}, f32[3,64,2048]{2,1,0:T(8,128)})) %all-reduce.3.cloned.1.call-update) | async-done | bytes 3014672 | tf_op jit(solution)/shard_map/psum | solution.py:322
  644.8 2.7 copy.296
  (519 shorter events, 204.1 us)
Async XLA Ops:
  7.2 10.8 %collective-permute-start.4 = (s32[1,16]{1,0:T(1,128)}, s32[1,16]{1,0:T(1,128)S(1)}, u32[]{:S(2)}, u32[]{:S(2)}) collective-permute-start(s32[1,16]{1,0:T(1,128)} %param.19), channel_id=1, source_target_pairs={{0,2},{2,0},{1,3},{3,1},{4,6},{6,4},{5,7},{7,5},{8,10},{10,8},{9,1... | collective-permute-start | bytes 200 | tf_op jit(solution)/shard_map/ppermute | solution.py:41
  10.2 5.8 collective-permute-start.3
  11.5 27.8 %collective-permute-start = (bf16[128,2048]{0,1:T(8,128)(2,1)S(1)}, bf16[128,2048]{0,1:T(8,128)(2,1)}, u32[]{:S(2)}, u32[]{:S(2)}) collective-permute-start(bf16[128,2048]{0,1:T(8,128)(2,1)S(1)} %bitcast.539), channel_id=1, source_target_pairs={{0,1},{1,0},{2,3},{3,2},{4,5},{5,4},{6,7},{7,6},{8,9},{9,8},{10,11... | collective-permute-start | bytes 1572872 | tf_op jit(solution)/shard_map/ppermute | solution.py:37
  12.1 26.7 %collective-permute-start.1 = (bf16[128,2048]{0,1:T(8,128)(2,1)S(1)}, bf16[128,2048]{0,1:T(8,128)(2,1)}, u32[]{:S(2)}, u32[]{:S(2)}) collective-permute-start(bf16[128,2048]{0,1:T(8,128)(2,1)S(1)} %bitcast.540), channel_id=1, source_target_pairs={{0,2},{2,0},{1,3},{3,1},{4,6},{6,4},{5,7},{7,5},{8,10},{10,8},{9,1... | collective-permute-start | bytes 1572872 | tf_op jit(solution)/shard_map/ppermute | solution.py:41
  14.7 21.3 %collective-permute-start.6 = (bf16[7,64,512]{2,1,0:T(8,128)(2,1)}, bf16[7,64,512]{2,1,0:T(8,128)(2,1)S(1)}, u32[]{:S(2)}, u32[]{:S(2)}) collective-permute-start(bf16[7,64,512]{2,1,0:T(8,128)(2,1)} %get-tuple-element.59), channel_id=1, source_target_pairs={{0,1},{1,0},{2,3},{3,2},{4,5},{5,4},{6,7},{7,6},{8,9},{9,8},{10,11... | collective-permute-start | bytes 1376264 | tf_op jit(solution)/shard_map/ppermute | solution.py:37
  16.0 20.0 %collective-permute-start.7 = (bf16[7,64,512]{2,1,0:T(8,128)(2,1)}, bf16[7,64,512]{2,1,0:T(8,128)(2,1)}, u32[]{:S(2)}, u32[]{:S(2)}) collective-permute-start(bf16[7,64,512]{2,1,0:T(8,128)(2,1)} %get-tuple-element.59), channel_id=1, source_target_pairs={{0,2},{2,0},{1,3},{3,1},{4,6},{6,4},{5,7},{7,5},{8,10},{10,8},{9,1... | collective-permute-start | bytes 1376264 | tf_op jit(solution)/shard_map/ppermute | solution.py:41
  36.0 5.8 collective-permute-start.8
  38.8 3.8 collective-permute-start.2
  54.0 4.3 collective-permute-start.10
  72.2 43.5 %all-to-all-start = ((bf16[8,3,128,256]{3,2,1,0:T(8,128)(2,1)}), bf16[8,3,128,256]{3,2,1,0:T(8,128)(2,1)}, u32[]{:S(2)}, u32[]{:S(2)}) async-start(bf16[8,3,128,256]{3,2,1,0:T(8,128)(2,1)} %bitcast.528), calls=%async_computation | async-start | bytes 3145728 | tf_op jit(solution)/shard_map/all_to_all | solution.py:173
  162.8 12.7 %collective-permute-start.12 = (bf16[512,512]{0,1:T(8,128)(2,1)S(1)}, bf16[512,512]{0,1:T(8,128)(2,1)S(1)}, u32[]{:S(2)}, u32[]{:S(2)}) collective-permute-start(bf16[512,512]{0,1:T(8,128)(2,1)S(1)} %bitcast.553), channel_id=1, source_target_pairs={{0,2},{2,0},{1,3},{3,1},{4,6},{6,4},{5,7},{7,5},{8,10},{10,8},{9,1... | collective-permute-start | bytes 1572872 | tf_op jit(solution)/shard_map/ppermute | solution.py:41
  164.5 11.3 %collective-permute-start.11 = (bf16[512,512]{0,1:T(8,128)(2,1)S(1)}, bf16[512,512]{0,1:T(8,128)(2,1)S(1)}, u32[]{:S(2)}, u32[]{:S(2)}) collective-permute-start(bf16[512,512]{0,1:T(8,128)(2,1)S(1)} %bitcast.554), channel_id=1, source_target_pairs={{0,1},{1,0},{2,3},{3,2},{4,5},{5,4},{6,7},{7,6},{8,9},{9,8},{10,11... | collective-permute-start | bytes 1572872 | tf_op jit(solution)/shard_map/ppermute | solution.py:37
  183.4 3.6 collective-permute-start.15
  188.2 12.8 %collective-permute-start.17 = (bf16[512,512]{0,1:T(8,128)(2,1)S(1)}, bf16[512,512]{0,1:T(8,128)(2,1)S(1)}, u32[]{:S(2)}, u32[]{:S(2)}) collective-permute-start(bf16[512,512]{0,1:T(8,128)(2,1)S(1)} %get-tuple-element.35), channel_id=1, source_target_pairs={{0,2},{2,0},{1,3},{3,1},{4,6},{6,4},{5,7},{7,5},{8,10},{10,8},{9,1... | collective-permute-start | bytes 1572872 | tf_op jit(solution)/shard_map/ppermute | solution.py:41
  189.8 11.3 %collective-permute-start.16 = (bf16[512,512]{0,1:T(8,128)(2,1)S(1)}, bf16[512,512]{0,1:T(8,128)(2,1)S(1)}, u32[]{:S(2)}, u32[]{:S(2)}) collective-permute-start(bf16[512,512]{0,1:T(8,128)(2,1)S(1)} %get-tuple-element.35), channel_id=1, source_target_pairs={{0,1},{1,0},{2,3},{3,2},{4,5},{5,4},{6,7},{7,6},{8,9},{9,8},{10,11... | collective-permute-start | bytes 1572872 | tf_op jit(solution)/shard_map/ppermute | solution.py:37
  242.9 19.3 %collective-permute-start.19 = (bf16[128,2048]{0,1:T(8,128)(2,1)}, bf16[128,2048]{0,1:T(8,128)(2,1)}, u32[]{:S(2)}, u32[]{:S(2)}) collective-permute-start(bf16[128,2048]{0,1:T(8,128)(2,1)} %get-tuple-element.46), channel_id=1, source_target_pairs={{0,1},{1,0},{2,3},{3,2},{4,5},{5,4},{6,7},{7,6},{8,9},{9,8},{10,11... | collective-permute-start | bytes 1572872 | tf_op jit(solution)/shard_map/ppermute | solution.py:37
  245.6 16.6 %collective-permute-start.21 = (bf16[128,2048]{0,1:T(8,128)(2,1)}, bf16[128,2048]{0,1:T(8,128)(2,1)}, u32[]{:S(2)}, u32[]{:S(2)}) collective-permute-start(bf16[128,2048]{0,1:T(8,128)(2,1)} %add_convert_fusion.8), channel_id=1, source_target_pairs={{0,2},{2,0},{1,3},{3,1},{4,6},{6,4},{5,7},{7,5},{8,10},{10,8},{9,1... | collective-permute-start | bytes 1572872 | tf_op jit(solution)/shard_map/ppermute | solution.py:41
  247.2 12.7 %collective-permute-start.23 = (bf16[1,512]{1,0:T(2,128)(2,1)S(1)}, bf16[1,512]{1,0:T(2,128)(2,1)S(1)}, u32[]{:S(2)}, u32[]{:S(2)}) collective-permute-start(bf16[1,512]{1,0:T(2,128)(2,1)S(1)} %get-tuple-element.78), channel_id=1, source_target_pairs={{0,2},{2,0},{1,3},{3,1},{4,6},{6,4},{5,7},{7,5},{8,10},{10,8},{9,1... | collective-permute-start | bytes 3080 | tf_op jit(solution)/shard_map/ppermute | solution.py:41
  247.7 13.6 %collective-permute-start.22 = (bf16[1,512]{1,0:T(2,128)(2,1)S(1)}, bf16[1,512]{1,0:T(2,128)(2,1)S(1)}, u32[]{:S(2)}, u32[]{:S(2)}) collective-permute-start(bf16[1,512]{1,0:T(2,128)(2,1)S(1)} %get-tuple-element.78), channel_id=1, source_target_pairs={{0,1},{1,0},{2,3},{3,2},{4,5},{5,4},{6,7},{7,6},{8,9},{9,8},{10,11... | collective-permute-start | bytes 3080 | tf_op jit(solution)/shard_map/ppermute | solution.py:37
  259.9 2.0 collective-permute-start.24
  266.0 14.4 %collective-permute-start.26 = (bf16[128,2048]{0,1:T(8,128)(2,1)S(1)}, bf16[128,2048]{0,1:T(8,128)(2,1)S(1)}, u32[]{:S(2)}, u32[]{:S(2)}) collective-permute-start(bf16[128,2048]{0,1:T(8,128)(2,1)S(1)} %get-tuple-element.33), channel_id=1, source_target_pairs={{0,2},{2,0},{1,3},{3,1},{4,6},{6,4},{5,7},{7,5},{8,10},{10,8},{9,1... | collective-permute-start | bytes 1572872 | tf_op jit(solution)/shard_map/ppermute | solution.py:41
  267.7 12.8 %collective-permute-start.25 = (bf16[128,2048]{0,1:T(8,128)(2,1)S(1)}, bf16[128,2048]{0,1:T(8,128)(2,1)S(1)}, u32[]{:S(2)}, u32[]{:S(2)}) collective-permute-start(bf16[128,2048]{0,1:T(8,128)(2,1)S(1)} %get-tuple-element.33), channel_id=1, source_target_pairs={{0,1},{1,0},{2,3},{3,2},{4,5},{5,4},{6,7},{7,6},{8,9},{9,8},{10,11... | collective-permute-start | bytes 1572872 | tf_op jit(solution)/shard_map/ppermute | solution.py:37
  315.6 2.0 collective-permute-start.29
  315.8 3.6 collective-permute-start.28
  317.7 14.0 %collective-permute-start.30 = (bf16[512,512]{0,1:T(8,128)(2,1)S(1)}, bf16[512,512]{0,1:T(8,128)(2,1)S(1)}, u32[]{:S(2)}, u32[]{:S(2)}) collective-permute-start(bf16[512,512]{0,1:T(8,128)(2,1)S(1)} %add_convert_fusion.6), channel_id=1, source_target_pairs={{0,2},{2,0},{1,3},{3,1},{4,6},{6,4},{5,7},{7,5},{8,10},{10,8},{9,1... | collective-permute-start | bytes 1572872 | tf_op jit(solution)/shard_map/ppermute | solution.py:41
  333.4 3.6 collective-permute-start.32
  342.2 2.0 collective-permute-start.34
  342.3 3.7 collective-permute-start.33
  344.4 14.0 %collective-permute-start.35 = (bf16[512,512]{1,0:T(8,128)(2,1)S(1)}, bf16[512,512]{1,0:T(8,128)(2,1)S(1)}, u32[]{:S(2)}, u32[]{:S(2)}) collective-permute-start(bf16[512,512]{1,0:T(8,128)(2,1)S(1)} %add_convert_fusion.5), channel_id=1, source_target_pairs={{0,2},{2,0},{1,3},{3,1},{4,6},{6,4},{5,7},{7,5},{8,10},{10,8},{9,1... | collective-permute-start | bytes 1572872 | tf_op jit(solution)/shard_map/ppermute | solution.py:41
  407.2 40.6 %all-to-all-start.3 = ((bf16[8,3,128,256]{2,3,1,0:T(8,128)(2,1)}), bf16[8,3,128,256]{2,3,1,0:T(8,128)(2,1)}, u32[]{:S(2)}, u32[]{:S(2)}) async-start(bf16[8,3,128,256]{2,3,1,0:T(8,128)(2,1)} %copy.187), calls=%async_computation.3 | async-start | bytes 3145728 | tf_op jit(solution)/shard_map/all_to_all | solution.py:180
  411.7 233.1 %all-reduce.3.cloned.1.call-start = ((), (), s32[]{:S(2)}) async-start(), calls=%async_computation.4 | async-start | bytes 6029312 | tf_op jit(solution)/shard_map/psum | solution.py:322
  414.0 3.9 collective-permute-start.54
  419.1 7.9 %collective-permute-start.51 = (f32[512,16]{0,1:T(8,128)}, f32[512,16]{0,1:T(8,128)}, u32[]{:S(2)}, u32[]{:S(2)}) collective-permute-start(f32[512,16]{0,1:T(8,128)} %reduce_sum.168), channel_id=1, source_target_pairs={{0,1},{1,0},{2,3},{3,2},{4,5},{5,4},{6,7},{7,6},{8,9},{9,8},{10,11... | collective-permute-start | bytes 98312 | tf_op jit(solution)/shard_map/ppermute | solution.py:37
  419.1 10.3 %collective-permute-start.49 = (f32[512,16]{0,1:T(8,128)S(1)}, f32[512,16]{0,1:T(8,128)S(1)}, u32[]{:S(2)}, u32[]{:S(2)}) collective-permute-start(f32[512,16]{0,1:T(8,128)S(1)} %reduce_sum.167), channel_id=1, source_target_pairs={{0,1},{1,0},{2,3},{3,2},{4,5},{5,4},{6,7},{7,6},{8,9},{9,8},{10,11... | collective-permute-start | bytes 98312 | tf_op jit(solution)/shard_map/ppermute | solution.py:37
  424.5 5.5 collective-permute-start.47
  427.9 6.1 collective-permute-start.52
  429.5 5.1 collective-permute-start.50
  430.0 12.5 %collective-permute-start.48 = (f32[512,16]{0,1:T(8,128)S(1)}, f32[512,16]{0,1:T(8,128)S(1)}, u32[]{:S(2)}, u32[]{:S(2)}) collective-permute-start(f32[512,16]{0,1:T(8,128)S(1)} %add.424), channel_id=1, source_target_pairs={{0,2},{2,0},{1,3},{3,1},{4,6},{6,4},{5,7},{7,5},{8,10},{10,8},{9,1... | collective-permute-start | bytes 98312 | tf_op jit(solution)/shard_map/ppermute | solution.py:41
  469.9 5.1 collective-permute-start.36
  475.0 3.7 collective-permute-start.37
  477.6 22.5 %collective-permute-start.45 = (f32[512,16]{0,1:T(8,128)}, f32[512,16]{0,1:T(8,128)}, u32[]{:S(2)}, u32[]{:S(2)}) collective-permute-start(f32[512,16]{0,1:T(8,128)} %reduce_sum.165), channel_id=1, source_target_pairs={{0,1},{1,0},{2,3},{3,2},{4,5},{5,4},{6,7},{7,6},{8,9},{9,8},{10,11... | collective-permute-start | bytes 98312 | tf_op jit(solution)/shard_map/ppermute | solution.py:37
  494.2 8.2 %collective-permute-start.43 = (f32[512,16]{0,1:T(8,128)}, f32[512,16]{0,1:T(8,128)}, u32[]{:S(2)}, u32[]{:S(2)}) collective-permute-start(f32[512,16]{0,1:T(8,128)} %reduce_sum.164), channel_id=1, source_target_pairs={{0,1},{1,0},{2,3},{3,2},{4,5},{5,4},{6,7},{7,6},{8,9},{9,8},{10,11... | collective-permute-start | bytes 98312 | tf_op jit(solution)/shard_map/ppermute | solution.py:37
  495.7 7.9 %collective-permute-start.41 = (f32[512,16]{0,1:T(8,128)}, f32[512,16]{0,1:T(8,128)S(1)}, u32[]{:S(2)}, u32[]{:S(2)}) collective-permute-start(f32[512,16]{0,1:T(8,128)} %reduce_sum.163), channel_id=1, source_target_pairs={{0,1},{1,0},{2,3},{3,2},{4,5},{5,4},{6,7},{7,6},{8,9},{9,8},{10,11... | collective-permute-start | bytes 98312 | tf_op jit(solution)/shard_map/ppermute | solution.py:37
  500.8 8.2 %collective-permute-start.46 = (f32[512,16]{0,1:T(8,128)S(1)}, f32[512,16]{0,1:T(8,128)S(1)}, u32[]{:S(2)}, u32[]{:S(2)}) collective-permute-start(f32[512,16]{0,1:T(8,128)S(1)} %add.422), channel_id=1, source_target_pairs={{0,2},{2,0},{1,3},{3,1},{4,6},{6,4},{5,7},{7,5},{8,10},{10,8},{9,1... | collective-permute-start | bytes 98312 | tf_op jit(solution)/shard_map/ppermute | solution.py:41
  503.1 5.9 collective-permute-start.44
  503.6 5.4 collective-permute-start.42
  532.2 5.5 collective-permute-start.38
  534.3 14.1 %collective-permute-start.40 = (bf16[128,2048]{1,0:T(8,128)(2,1)S(1)}, bf16[128,2048]{1,0:T(8,128)(2,1)}, u32[]{:S(2)}, u32[]{:S(2)}) collective-permute-start(bf16[128,2048]{1,0:T(8,128)(2,1)S(1)} %add_convert_fusion.3), channel_id=1, source_target_pairs={{0,2},{2,0},{1,3},{3,1},{4,6},{6,4},{5,7},{7,5},{8,10},{10,8},{9,1... | collective-permute-start | bytes 1572872 | tf_op jit(solution)/shard_map/ppermute | solution.py:41
  (117 other events, 1054.9 us)
Sparse Core Ops, SparseCore 0:
  520.7 124.0 all-reduce.2
where the time goes:
time: 666 us; the launch traced here: 656 us
  waiting for transfers between devices  250 us (38%)
  matrix products  167 us (25%)
  local copies, waits for them, and re-layouts  87.8 us (13%)
  other arithmetic  51.1 us (8%)
  starting transfers between devices  46.8 us (7%)
  blocking collectives  37 us (6%)
  between operations  16.2 us (2%)
    dot_general x56, matrix products, dot(): lax.dot_general(left, right, (dims, ((), ())), preferred_element_type=F32)  145 us
    ppermute x22, waiting for transfers between devices, swap_chip(): return lax.ppermute(values, 'wsh', CHIP_SWAP)  102 us
    psum x1, waiting for transfers between devices, per_device(): model_grads = lax.psum(model_grads, 'ctx')  93.8 us
    all_to_all x1, waiting for transfers between devices, to_heads(): lax.all_to_all(shaped, 'ctx', 0, 0, tiled=True, axis_index_groups=ctx_gro...  34 us
    ppermute x22, starting transfers between devices, swap_chip(): return lax.ppermute(values, 'wsh', CHIP_SWAP)  30 us
    unnamed x222, local copies, waits for them, and re-layouts  22.5 us
    dot_general x6, matrix products, batched(): lax.dot_general(left, right, (((lc,), (rc,)), ((0,), (0,))), preferred_el...  21.8 us
    all_to_all x1, blocking collectives, to_heads(): lax.all_to_all(shaped, 'ctx', 0, 0, tiled=True, axis_index_groups=ctx_gro...  18.6 us
  transfers between devices with their start and end apart: 58, of which 27 were waited for; matrix products, arithmetic and copies ran while one was open for 15% of the time, Pallas kernels for 0%

commit v1 on v0

--- a/solution.py
+++ b/solution.py
@@ -319,7 +319,7 @@
     model_grads = jnp.stack(
         grad_a_in + [grad_a_out, grad_a_gate, grad_a_up] + grad_b_in + [grad_b_out, grad_b_down]
     )
-    model_grads = lax.psum(model_grads, "ctx")
+    model_grads = jnp.sum(lax.all_gather(model_grads, "ctx"), axis=0)
     hidden_grads = lax.psum(hidden_grads, "ctx")
     return (result.astype(BF16)[None], grad_inputs[None], model_grads, hidden_grads)
 

time: 666 us -> 781 us (1.17)
  waiting for transfers between devices: 250 us -> 383 us
  matrix products: 167 us -> 141 us
  other arithmetic: 51.1 us -> 66.2 us
    all_gather x0 -> x1, waiting for transfers between devices: none -> 116 us  [per_device(): model_grads = jnp.sum(lax.all_gather(model_grads, 'ctx'), axis=0)]
    all_to_all x1, waiting for transfers between devices: 4.69 us -> 32 us  [to_rows(): lax.all_to_all(shaped.transpose(1, 0, 2, 3), 'ctx', 0, 0, tiled=True, axi...]
    dot_general x56, matrix products: 145 us -> 120 us  [dot(): lax.dot_general(left, right, (dims, ((), ())), preferred_element_type=F32)]
    psum x1, waiting for transfers between devices: 93.8 us -> 84.6 us  [per_device(): hidden_grads = lax.psum(hidden_grads, 'ctx')]
    unnamed x222 -> x211, local copies, waits for them, and re-layouts: 22.5 us -> 20.8 us
  transfers between devices with their start and end apart: 58 -> 59, of which waited for: 27 -> 27; matrix products, arithmetic and copies ran while one was open for 15% -> 14% of each run, Pallas kernels for 0% -> 0%
where the time goes in v1:
time: 781 us; the launch traced here: 770 us
  waiting for transfers between devices  383 us (49%)
  matrix products  141 us (18%)
  local copies, waits for them, and re-layouts  81 us (10%)
  other arithmetic  66.2 us (8%)
  starting transfers between devices  45.8 us (6%)
  blocking collectives  36.8 us (5%)
  between operations  16.2 us (2%)
    dot_general x56, matrix products, dot(): lax.dot_general(left, right, (dims, ((), ())), preferred_element_type=F32)  120 us
    all_gather x1, waiting for transfers between devices, per_device(): model_grads = jnp.sum(lax.all_gather(model_grads, 'ctx'), axis=0)  116 us
    ppermute x22, waiting for transfers between devices, swap_chip(): return lax.ppermute(values, 'wsh', CHIP_SWAP)  103 us
    psum x1, waiting for transfers between devices, per_device(): hidden_grads = lax.psum(hidden_grads, 'ctx')  84.6 us
    all_to_all x1, waiting for transfers between devices, to_heads(): lax.all_to_all(shaped, 'ctx', 0, 0, tiled=True, axis_index_groups=ctx_gro...  34 us
    all_to_all x1, waiting for transfers between devices, to_rows(): lax.all_to_all(shaped.transpose(1, 0, 2, 3), 'ctx', 0, 0, tiled=True, axi...  32 us
    ppermute x22, starting transfers between devices, swap_chip(): return lax.ppermute(values, 'wsh', CHIP_SWAP)  29.5 us
    dot_general x6, matrix products, batched(): lax.dot_general(left, right, (((lc,), (rc,)), ((0,), (0,))), preferred_el...  21.8 us
  transfers between devices with their start and end apart: 59, of which 27 were waited for; matrix products, arithmetic and copies ran while one was open for 14% of the time, Pallas kernels for 0%

profile of v1, /device:TPU:0, one launch (start us, length us, event | category | flops | bytes accessed | tf_op | source)
XLA Modules:
  0.0 769.9 jit_solution(15394064448804835944)
XLA Ops:
  7.2 3.0 collective-permute-start.4
  19.7 16.3 %collective-permute-done.7 = bf16[7,64,512]{2,1,0:T(8,128)(2,1)} collective-permute-done((bf16[7,64,512]{2,1,0:T(8,128)(2,1)}, bf16[7,64,512]{2,1,0:T(8,128)(2,1)}, u32[]{:S(2)}, u32[]{:S(2)}) %collective-permute-start.7) | collective-permute-done | bytes 458784 | tf_op jit(solution)/shard_map/ppermute | solution.py:41
  64.4 3.7 maximum_bitcast_fusion
  68.1 3.7 copy.160
  71.8 6.4 all-to-all-start
  81.3 34.0 %all-to-all-done = bf16[8,3,128,256]{3,2,1,0:T(8,128)(2,1)} async-done(((bf16[8,3,128,256]{3,2,1,0:T(8,128)(2,1)}), bf16[8,3,128,256]{3,2,1,0:T(8,128)(2,1)}, u32[]{:S(2)}, u32[]{:S(2)}) %all-to-all-start) | async-done | bytes 1572896 | tf_op jit(solution)/shard_map/all_to_all | solution.py:173
  115.3 2.8 copy.161
  118.1 3.7 reshape.481
  121.8 2.6 copy.162
  124.3 3.0 fusion.18
  130.6 4.8 fusion.75
  138.7 18.4 %all_to_all.20 = bf16[8,1,128,256]{2,3,1,0:T(8,128)(2,1)} all-to-all(bf16[8,1,128,256]{2,3,1,0:T(8,128)(2,1)S(1)} %copy.165), channel_id=1, replica_groups={{0,4,8,12,16,20,24,28},{1,5,9,13,17,21,25,29},{2,6,10,14,18,22,26,30},{..., dimensions={0} | all-to-all | bytes 1048576 | tf_op jit(solution)/shard_map/all_to_all | solution.py:180
  164.1 11.1 %collective-permute-done.12 = bf16[512,512]{0,1:T(8,128)(2,1)S(1)} collective-permute-done((bf16[512,512]{0,1:T(8,128)(2,1)S(1)}, bf16[512,512]{0,1:T(8,128)(2,1)S(1)}, u32[]{:S(2)}, u32[]{:S(2)}) %collective-permute-start.12) | collective-permute-done | bytes 524320 | tf_op jit(solution)/shard_map/ppermute | solution.py:41
  178.6 2.9 multiply_reduce_fusion.5
  189.0 11.3 %collective-permute-done.17 = bf16[512,512]{0,1:T(8,128)(2,1)S(1)} collective-permute-done((bf16[512,512]{0,1:T(8,128)(2,1)S(1)}, bf16[512,512]{0,1:T(8,128)(2,1)S(1)}, u32[]{:S(2)}, u32[]{:S(2)}) %collective-permute-start.17) | collective-permute-done | bytes 524320 | tf_op jit(solution)/shard_map/ppermute | solution.py:41
  205.6 11.6 %multiply_add_fusion.1 = f32[512,2048]{0,1:T(8,128)} fusion(f32[512,2048]{0,1:T(8,128)S(1)} %fusion.137, bf16[512,2048]{0,1:T(8,128)(2,1)S(1)} %constant_dynamic-update-slice_fusion.4, bf16[3,2048,2048]{2,1,0:T(8,128)(2,1)} %param.13), kind=kOutput, calls=%fused_computation.37 | convolution fusion | flops 4297064448 | bytes 18874368 | tf_op jit(solution)/shard_map/dot_general | solution.py:21
  217.1 13.1 %multiply_convert_fusion.3 = (bf16[512,2048]{0,1:T(8,128)(2,1)S(1)}, f32[512,2048]{0,1:T(8,128)}) fusion(f32[512,2048]{0,1:T(8,128)} %multiply_add_fusion.1, f32[512,2048]{0,1:T(8,128)S(1)} %fusion.134, bf16[512,2048]{0,1:T(8,128)(2,1)S(1)} %constant_dynamic-update-slice_fusion.4, bf16[3,2048,2048]{2,1,0:T(8,128)(2,1)} %param.13), kind=kOutput, calls=%fused_computation.33 | convolution fusion | flops 4303355904 | bytes 25165824 | tf_op jit(solution)/shard_map/dot_general | solution.py:21
  230.7 7.2 fusion.2
  247.1 10.0 %collective-permute-done.23 = bf16[1,512]{1,0:T(2,128)(2,1)S(1)} collective-permute-done((bf16[1,512]{1,0:T(2,128)(2,1)S(1)}, bf16[1,512]{1,0:T(2,128)(2,1)S(1)}, u32[]{:S(2)}, u32[]{:S(2)}) %collective-permute-start.23) | collective-permute-done | bytes 1056 | tf_op jit(solution)/shard_map/ppermute | solution.py:41
  265.4 12.5 %collective-permute-done.26 = bf16[128,2048]{0,1:T(8,128)(2,1)S(1)} collective-permute-done((bf16[128,2048]{0,1:T(8,128)(2,1)S(1)}, bf16[128,2048]{0,1:T(8,128)(2,1)S(1)}, u32[]{:S(2)}, u32[]{:S(2)}) %collective-permute-start.26) | collective-permute-done | bytes 524320 | tf_op jit(solution)/shard_map/ppermute | solution.py:41
  281.3 9.9 %multiply_convert_fusion.1 = (bf16[512,2048]{0,1:T(8,128)(2,1)S(1)}, bf16[512,2048]{0,1:T(8,128)(2,1)S(1)}) fusion(f32[512,2048]{0,1:T(8,128)} %multiply_add_fusion.1, f32[512,2048]{0,1:T(8,128)} %get-tuple-element.94, f32[512,2048]{0,1:T(8,128)S(1)} %fusion.130, bf16[512,2048]{0,1:T(8,128)(2,1)S(1)} %constant_dynamic-update-slice_fusion, ...), kind=kOutput, calls=%fused_computation.30 | convolution fusion | flops 4309647360 | bytes 27262976 | tf_op jit(solution)/shard_map/dot_general | solution.py:21
  291.7 7.9 %fusion.8 = f32[512,2048]{0,1:T(8,128)S(1)} fusion(bf16[512,2048]{0,1:T(8,128)(2,1)S(1)} %get-tuple-element.37, bf16[3,2048,2048]{2,1,0:T(8,128)(2,1)} %param.13), kind=kOutput, calls=%fused_computation.8 | convolution fusion | flops 4294967296 | bytes 14680064 | tf_op jit(solution)/shard_map/dot_general | solution.py:21
  300.1 6.9 fusion.4
  313.9 12.4 %collective-permute-done.30 = bf16[512,512]{0,1:T(8,128)(2,1)S(1)} collective-permute-done((bf16[512,512]{0,1:T(8,128)(2,1)S(1)}, bf16[512,512]{0,1:T(8,128)(2,1)S(1)}, u32[]{:S(2)}, u32[]{:S(2)}) %collective-permute-start.30) | collective-permute-done | bytes 524320 | tf_op jit(solution)/shard_map/ppermute | solution.py:41
  332.0 3.0 fusion.32
  339.6 12.4 %collective-permute-done.35 = bf16[512,512]{1,0:T(8,128)(2,1)S(1)} collective-permute-done((bf16[512,512]{1,0:T(8,128)(2,1)S(1)}, bf16[512,512]{1,0:T(8,128)(2,1)S(1)}, u32[]{:S(2)}, u32[]{:S(2)}) %collective-permute-start.35) | collective-permute-done | bytes 524320 | tf_op jit(solution)/shard_map/ppermute | solution.py:41
  356.2 18.4 %all_to_all.21 = bf16[8,1,128,256]{3,2,1,0:T(8,128)(2,1)} all-to-all(bf16[8,1,128,256]{3,2,1,0:T(8,128)(2,1)S(1)} %bitcast.548), channel_id=1, replica_groups={{0,4,8,12,16,20,24,28},{1,5,9,13,17,21,25,29},{2,6,10,14,18,22,26,30},{..., dimensions={0} | all-to-all | bytes 1048576 | tf_op jit(solution)/shard_map/all_to_all | solution.py:173
  376.5 5.5 fusion.76
  382.1 5.5 multiply_reduce_fusion
  387.6 2.7 multiply_convert_fusion
  394.7 2.6 copy.186
  400.6 4.4 all-to-all-start.3
  409.2 32.0 %all-to-all-done.3 = bf16[8,3,128,256]{2,3,1,0:T(8,128)(2,1)} async-done(((bf16[8,3,128,256]{2,3,1,0:T(8,128)(2,1)}), bf16[8,3,128,256]{2,3,1,0:T(8,128)(2,1)}, u32[]{:S(2)}, u32[]{:S(2)}) %all-to-all-start.3) | async-done | bytes 1572896 | tf_op jit(solution)/shard_map/all_to_all | solution.py:180
  441.2 3.0 copy.188
  444.1 2.7 fusion.192
  449.8 2.6 copy.189
  452.4 2.6 reshape.498
  506.5 3.2 convolution_bitcast_fusion
  509.7 3.1 fusion.31
  515.9 3.0 fusion.36
  520.8 3.6 fusion.140
  527.1 4.3 add_convert_fusion
  540.1 9.8 %collective-permute-done.40 = bf16[128,2048]{1,0:T(8,128)(2,1)} collective-permute-done((bf16[128,2048]{1,0:T(8,128)(2,1)S(1)}, bf16[128,2048]{1,0:T(8,128)(2,1)}, u32[]{:S(2)}, u32[]{:S(2)}) %collective-permute-start.40) | collective-permute-done | bytes 524320 | tf_op jit(solution)/shard_map/ppermute | solution.py:41
  550.0 2.4 add_bitcast_fusion
  552.4 116.2 %all-gather.3.cloned.1.call-done = f32[88,64,512]{2,1,0:T(8,128)} async-done(((f32[11,64,512]{2,1,0:T(8,128)}), f32[88,64,512]{2,1,0:T(8,128)}) %all-gather.3.cloned.1.call-update) | async-done | bytes 11534352 | tf_op jit(solution)/shard_map/all_gather | solution.py:322
  668.6 6.9 reduce_sum.179
  675.5 84.6 %all-reduce.2.cloned.1.call-done = f32[3,64,2048]{2,1,0:T(8,128)} async-done(((f32[3,64,2048]{2,1,0:T(8,128)}), f32[3,64,2048]{2,1,0:T(8,128)}) %all-reduce.2.cloned.1.call-update) | async-done | bytes 1572880 | tf_op jit(solution)/shard_map/psum | solution.py:323
  760.1 2.7 copy.295
  (513 shorter events, 197.3 us)
Async XLA Ops:
  7.2 9.8 %collective-permute-start.4 = (s32[1,16]{1,0:T(1,128)}, s32[1,16]{1,0:T(1,128)S(1)}, u32[]{:S(2)}, u32[]{:S(2)}) collective-permute-start(s32[1,16]{1,0:T(1,128)} %param.19), channel_id=1, source_target_pairs={{0,2},{2,0},{1,3},{3,1},{4,6},{6,4},{5,7},{7,5},{8,10},{10,8},{9,1... | collective-permute-start | bytes 200 | tf_op jit(solution)/shard_map/ppermute | solution.py:41
  10.2 4.7 collective-permute-start.3
  11.5 27.8 %collective-permute-start = (bf16[128,2048]{0,1:T(8,128)(2,1)S(1)}, bf16[128,2048]{0,1:T(8,128)(2,1)}, u32[]{:S(2)}, u32[]{:S(2)}) collective-permute-start(bf16[128,2048]{0,1:T(8,128)(2,1)S(1)} %bitcast.543), channel_id=1, source_target_pairs={{0,1},{1,0},{2,3},{3,2},{4,5},{5,4},{6,7},{7,6},{8,9},{9,8},{10,11... | collective-permute-start | bytes 1572872 | tf_op jit(solution)/shard_map/ppermute | solution.py:37
  12.1 26.7 %collective-permute-start.1 = (bf16[128,2048]{0,1:T(8,128)(2,1)S(1)}, bf16[128,2048]{0,1:T(8,128)(2,1)}, u32[]{:S(2)}, u32[]{:S(2)}) collective-permute-start(bf16[128,2048]{0,1:T(8,128)(2,1)S(1)} %bitcast.544), channel_id=1, source_target_pairs={{0,2},{2,0},{1,3},{3,1},{4,6},{6,4},{5,7},{7,5},{8,10},{10,8},{9,1... | collective-permute-start | bytes 1572872 | tf_op jit(solution)/shard_map/ppermute | solution.py:41
  13.3 22.6 %collective-permute-start.6 = (bf16[7,64,512]{2,1,0:T(8,128)(2,1)}, bf16[7,64,512]{2,1,0:T(8,128)(2,1)S(1)}, u32[]{:S(2)}, u32[]{:S(2)}) collective-permute-start(bf16[7,64,512]{2,1,0:T(8,128)(2,1)} %get-tuple-element.57), channel_id=1, source_target_pairs={{0,1},{1,0},{2,3},{3,2},{4,5},{5,4},{6,7},{7,6},{8,9},{9,8},{10,11... | collective-permute-start | bytes 1376264 | tf_op jit(solution)/shard_map/ppermute | solution.py:37
  14.9 21.0 %collective-permute-start.7 = (bf16[7,64,512]{2,1,0:T(8,128)(2,1)}, bf16[7,64,512]{2,1,0:T(8,128)(2,1)}, u32[]{:S(2)}, u32[]{:S(2)}) collective-permute-start(bf16[7,64,512]{2,1,0:T(8,128)(2,1)} %get-tuple-element.57), channel_id=1, source_target_pairs={{0,2},{2,0},{1,3},{3,1},{4,6},{6,4},{5,7},{7,5},{8,10},{10,8},{9,1... | collective-permute-start | bytes 1376264 | tf_op jit(solution)/shard_map/ppermute | solution.py:41
  36.0 5.7 collective-permute-start.8
  38.8 3.7 collective-permute-start.2
  53.6 4.3 collective-permute-start.10
  71.8 43.5 %all-to-all-start = ((bf16[8,3,128,256]{3,2,1,0:T(8,128)(2,1)}), bf16[8,3,128,256]{3,2,1,0:T(8,128)(2,1)}, u32[]{:S(2)}, u32[]{:S(2)}) async-start(bf16[8,3,128,256]{3,2,1,0:T(8,128)(2,1)} %bitcast.532), calls=%async_computation | async-start | bytes 3145728 | tf_op jit(solution)/shard_map/all_to_all | solution.py:173
  162.5 12.7 %collective-permute-start.12 = (bf16[512,512]{0,1:T(8,128)(2,1)S(1)}, bf16[512,512]{0,1:T(8,128)(2,1)S(1)}, u32[]{:S(2)}, u32[]{:S(2)}) collective-permute-start(bf16[512,512]{0,1:T(8,128)(2,1)S(1)} %bitcast.557), channel_id=1, source_target_pairs={{0,2},{2,0},{1,3},{3,1},{4,6},{6,4},{5,7},{7,5},{8,10},{10,8},{9,1... | collective-permute-start | bytes 1572872 | tf_op jit(solution)/shard_map/ppermute | solution.py:41
  164.1 11.3 %collective-permute-start.11 = (bf16[512,512]{0,1:T(8,128)(2,1)S(1)}, bf16[512,512]{0,1:T(8,128)(2,1)S(1)}, u32[]{:S(2)}, u32[]{:S(2)}) collective-permute-start(bf16[512,512]{0,1:T(8,128)(2,1)S(1)} %bitcast.558), channel_id=1, source_target_pairs={{0,1},{1,0},{2,3},{3,2},{4,5},{5,4},{6,7},{7,6},{8,9},{9,8},{10,11... | collective-permute-start | bytes 1572872 | tf_op jit(solution)/shard_map/ppermute | solution.py:37
  182.8 3.6 collective-permute-start.15
  187.5 12.9 %collective-permute-start.17 = (bf16[512,512]{0,1:T(8,128)(2,1)S(1)}, bf16[512,512]{0,1:T(8,128)(2,1)S(1)}, u32[]{:S(2)}, u32[]{:S(2)}) collective-permute-start(bf16[512,512]{0,1:T(8,128)(2,1)S(1)} %get-tuple-element.33), channel_id=1, source_target_pairs={{0,2},{2,0},{1,3},{3,1},{4,6},{6,4},{5,7},{7,5},{8,10},{10,8},{9,1... | collective-permute-start | bytes 1572872 | tf_op jit(solution)/shard_map/ppermute | solution.py:41
  189.0 11.3 %collective-permute-start.16 = (bf16[512,512]{0,1:T(8,128)(2,1)S(1)}, bf16[512,512]{0,1:T(8,128)(2,1)S(1)}, u32[]{:S(2)}, u32[]{:S(2)}) collective-permute-start(bf16[512,512]{0,1:T(8,128)(2,1)S(1)} %get-tuple-element.33), channel_id=1, source_target_pairs={{0,1},{1,0},{2,3},{3,2},{4,5},{5,4},{6,7},{7,6},{8,9},{9,8},{10,11... | collective-permute-start | bytes 1572872 | tf_op jit(solution)/shard_map/ppermute | solution.py:37
  240.0 19.4 %collective-permute-start.19 = (bf16[128,2048]{0,1:T(8,128)(2,1)}, bf16[128,2048]{0,1:T(8,128)(2,1)}, u32[]{:S(2)}, u32[]{:S(2)}) collective-permute-start(bf16[128,2048]{0,1:T(8,128)(2,1)} %get-tuple-element.44), channel_id=1, source_target_pairs={{0,1},{1,0},{2,3},{3,2},{4,5},{5,4},{6,7},{7,6},{8,9},{9,8},{10,11... | collective-permute-start | bytes 1572872 | tf_op jit(solution)/shard_map/ppermute | solution.py:37
  242.8 16.6 %collective-permute-start.21 = (bf16[128,2048]{0,1:T(8,128)(2,1)}, bf16[128,2048]{0,1:T(8,128)(2,1)}, u32[]{:S(2)}, u32[]{:S(2)}) collective-permute-start(bf16[128,2048]{0,1:T(8,128)(2,1)} %add_convert_fusion.8), channel_id=1, source_target_pairs={{0,2},{2,0},{1,3},{3,1},{4,6},{6,4},{5,7},{7,5},{8,10},{10,8},{9,1... | collective-permute-start | bytes 1572872 | tf_op jit(solution)/shard_map/ppermute | solution.py:41
  244.3 12.8 %collective-permute-start.23 = (bf16[1,512]{1,0:T(2,128)(2,1)S(1)}, bf16[1,512]{1,0:T(2,128)(2,1)S(1)}, u32[]{:S(2)}, u32[]{:S(2)}) collective-permute-start(bf16[1,512]{1,0:T(2,128)(2,1)S(1)} %get-tuple-element.76), channel_id=1, source_target_pairs={{0,2},{2,0},{1,3},{3,1},{4,6},{6,4},{5,7},{7,5},{8,10},{10,8},{9,1... | collective-permute-start | bytes 3080 | tf_op jit(solution)/shard_map/ppermute | solution.py:41
  244.9 13.6 %collective-permute-start.22 = (bf16[1,512]{1,0:T(2,128)(2,1)S(1)}, bf16[1,512]{1,0:T(2,128)(2,1)S(1)}, u32[]{:S(2)}, u32[]{:S(2)}) collective-permute-start(bf16[1,512]{1,0:T(2,128)(2,1)S(1)} %get-tuple-element.76), channel_id=1, source_target_pairs={{0,1},{1,0},{2,3},{3,2},{4,5},{5,4},{6,7},{7,6},{8,9},{9,8},{10,11... | collective-permute-start | bytes 3080 | tf_op jit(solution)/shard_map/ppermute | solution.py:37
  263.5 14.4 %collective-permute-start.26 = (bf16[128,2048]{0,1:T(8,128)(2,1)S(1)}, bf16[128,2048]{0,1:T(8,128)(2,1)S(1)}, u32[]{:S(2)}, u32[]{:S(2)}) collective-permute-start(bf16[128,2048]{0,1:T(8,128)(2,1)S(1)} %get-tuple-element.31), channel_id=1, source_target_pairs={{0,2},{2,0},{1,3},{3,1},{4,6},{6,4},{5,7},{7,5},{8,10},{10,8},{9,1... | collective-permute-start | bytes 1572872 | tf_op jit(solution)/shard_map/ppermute | solution.py:41
  265.1 12.9 %collective-permute-start.25 = (bf16[128,2048]{0,1:T(8,128)(2,1)S(1)}, bf16[128,2048]{0,1:T(8,128)(2,1)S(1)}, u32[]{:S(2)}, u32[]{:S(2)}) collective-permute-start(bf16[128,2048]{0,1:T(8,128)(2,1)S(1)} %get-tuple-element.31), channel_id=1, source_target_pairs={{0,1},{1,0},{2,3},{3,2},{4,5},{5,4},{6,7},{7,6},{8,9},{9,8},{10,11... | collective-permute-start | bytes 1572872 | tf_op jit(solution)/shard_map/ppermute | solution.py:37
  310.4 3.6 collective-permute-start.28
  312.3 14.0 %collective-permute-start.30 = (bf16[512,512]{0,1:T(8,128)(2,1)S(1)}, bf16[512,512]{0,1:T(8,128)(2,1)S(1)}, u32[]{:S(2)}, u32[]{:S(2)}) collective-permute-start(bf16[512,512]{0,1:T(8,128)(2,1)S(1)} %add_convert_fusion.6), channel_id=1, source_target_pairs={{0,2},{2,0},{1,3},{3,1},{4,6},{6,4},{5,7},{7,5},{8,10},{10,8},{9,1... | collective-permute-start | bytes 1572872 | tf_op jit(solution)/shard_map/ppermute | solution.py:41
  327.9 3.6 collective-permute-start.32
  335.9 3.7 collective-permute-start.33
  338.0 14.0 %collective-permute-start.35 = (bf16[512,512]{1,0:T(8,128)(2,1)S(1)}, bf16[512,512]{1,0:T(8,128)(2,1)S(1)}, u32[]{:S(2)}, u32[]{:S(2)}) collective-permute-start(bf16[512,512]{1,0:T(8,128)(2,1)S(1)} %add_convert_fusion.5), channel_id=1, source_target_pairs={{0,2},{2,0},{1,3},{3,1},{4,6},{6,4},{5,7},{7,5},{8,10},{10,8},{9,1... | collective-permute-start | bytes 1572872 | tf_op jit(solution)/shard_map/ppermute | solution.py:41
  400.6 40.6 %all-to-all-start.3 = ((bf16[8,3,128,256]{2,3,1,0:T(8,128)(2,1)}), bf16[8,3,128,256]{2,3,1,0:T(8,128)(2,1)}, u32[]{:S(2)}, u32[]{:S(2)}) async-start(bf16[8,3,128,256]{2,3,1,0:T(8,128)(2,1)} %copy.187), calls=%async_computation.3 | async-start | bytes 3145728 | tf_op jit(solution)/shard_map/all_to_all | solution.py:180
  405.0 263.5 %all-gather.3.cloned.1.call-start = ((), (), s32[]{:S(2)}) async-start(), calls=%async_computation.5 | async-start | bytes 12976128 | tf_op jit(solution)/shard_map/all_gather | solution.py:322
  406.3 53.9 %collective-permute-start.53 = (f32[512,16]{0,1:T(8,128)}, f32[512,16]{0,1:T(8,128)}, u32[]{:S(2)}, u32[]{:S(2)}) collective-permute-start(f32[512,16]{0,1:T(8,128)} %reduce_sum.178), channel_id=1, source_target_pairs={{0,1},{1,0},{2,3},{3,2},{4,5},{5,4},{6,7},{7,6},{8,9},{9,8},{10,11... | collective-permute-start | bytes 98312 | tf_op jit(solution)/shard_map/ppermute | solution.py:37
  406.9 56.3 %collective-permute-start.51 = (f32[512,16]{0,1:T(8,128)}, f32[512,16]{0,1:T(8,128)}, u32[]{:S(2)}, u32[]{:S(2)}) collective-permute-start(f32[512,16]{0,1:T(8,128)} %reduce_sum.177), channel_id=1, source_target_pairs={{0,1},{1,0},{2,3},{3,2},{4,5},{5,4},{6,7},{7,6},{8,9},{9,8},{10,11... | collective-permute-start | bytes 98312 | tf_op jit(solution)/shard_map/ppermute | solution.py:37
  408.0 57.0 %collective-permute-start.49 = (f32[512,16]{0,1:T(8,128)}, f32[512,16]{0,1:T(8,128)}, u32[]{:S(2)}, u32[]{:S(2)}) collective-permute-start(f32[512,16]{0,1:T(8,128)} %reduce_sum.176), channel_id=1, source_target_pairs={{0,1},{1,0},{2,3},{3,2},{4,5},{5,4},{6,7},{7,6},{8,9},{9,8},{10,11... | collective-permute-start | bytes 98312 | tf_op jit(solution)/shard_map/ppermute | solution.py:37
  408.7 59.3 %collective-permute-start.47 = (f32[512,16]{0,1:T(8,128)}, f32[512,16]{0,1:T(8,128)}, u32[]{:S(2)}, u32[]{:S(2)}) collective-permute-start(f32[512,16]{0,1:T(8,128)} %reduce_sum.175), channel_id=1, source_target_pairs={{0,1},{1,0},{2,3},{3,2},{4,5},{5,4},{6,7},{7,6},{8,9},{9,8},{10,11... | collective-permute-start | bytes 98312 | tf_op jit(solution)/shard_map/ppermute | solution.py:37
  459.6 10.9 %collective-permute-start.36 = (f32[2,512]{1,0:T(2,128)S(1)}, f32[2,512]{1,0:T(2,128)S(1)}, u32[]{:S(2)}, u32[]{:S(2)}) collective-permute-start(f32[2,512]{1,0:T(2,128)S(1)} %pad_maximum_fusion.7), channel_id=1, source_target_pairs={{0,1},{1,0},{2,3},{3,2},{4,5},{5,4},{6,7},{7,6},{8,9},{9,8},{10,11... | collective-permute-start | bytes 12296 | tf_op jit(solution)/shard_map/ppermute | solution.py:37
  461.6 18.8 %collective-permute-start.54 = (f32[512,16]{0,1:T(8,128)}, f32[512,16]{0,1:T(8,128)}, u32[]{:S(2)}, u32[]{:S(2)}) collective-permute-start(f32[512,16]{0,1:T(8,128)} %add.428), channel_id=1, source_target_pairs={{0,2},{2,0},{1,3},{3,1},{4,6},{6,4},{5,7},{7,5},{8,10},{10,8},{9,1... | collective-permute-start | bytes 98312 | tf_op jit(solution)/shard_map/ppermute | solution.py:41
  464.6 17.9 %collective-permute-start.52 = (f32[512,16]{0,1:T(8,128)}, f32[512,16]{0,1:T(8,128)}, u32[]{:S(2)}, u32[]{:S(2)}) collective-permute-start(f32[512,16]{0,1:T(8,128)} %add.426), channel_id=1, source_target_pairs={{0,2},{2,0},{1,3},{3,1},{4,6},{6,4},{5,7},{7,5},{8,10},{10,8},{9,1... | collective-permute-start | bytes 98312 | tf_op jit(solution)/shard_map/ppermute | solution.py:41
  466.4 18.3 %collective-permute-start.50 = (f32[512,16]{0,1:T(8,128)}, f32[512,16]{0,1:T(8,128)}, u32[]{:S(2)}, u32[]{:S(2)}) collective-permute-start(f32[512,16]{0,1:T(8,128)} %add.424), channel_id=1, source_target_pairs={{0,2},{2,0},{1,3},{3,1},{4,6},{6,4},{5,7},{7,5},{8,10},{10,8},{9,1... | collective-permute-start | bytes 98312 | tf_op jit(solution)/shard_map/ppermute | solution.py:41
  469.4 16.2 %collective-permute-start.48 = (f32[512,16]{0,1:T(8,128)}, f32[512,16]{0,1:T(8,128)}, u32[]{:S(2)}, u32[]{:S(2)}) collective-permute-start(f32[512,16]{0,1:T(8,128)} %add.422), channel_id=1, source_target_pairs={{0,2},{2,0},{1,3},{3,1},{4,6},{6,4},{5,7},{7,5},{8,10},{10,8},{9,1... | collective-permute-start | bytes 98312 | tf_op jit(solution)/shard_map/ppermute | solution.py:41
  470.5 3.7 collective-permute-start.37
  474.2 12.1 %collective-permute-start.45 = (f32[512,16]{0,1:T(8,128)}, f32[512,16]{0,1:T(8,128)}, u32[]{:S(2)}, u32[]{:S(2)}) collective-permute-start(f32[512,16]{0,1:T(8,128)} %reduce_sum.174), channel_id=1, source_target_pairs={{0,1},{1,0},{2,3},{3,2},{4,5},{5,4},{6,7},{7,6},{8,9},{9,8},{10,11... | collective-permute-start | bytes 98312 | tf_op jit(solution)/shard_map/ppermute | solution.py:37
  480.4 8.3 %collective-permute-start.43 = (f32[512,16]{0,1:T(8,128)}, f32[512,16]{0,1:T(8,128)}, u32[]{:S(2)}, u32[]{:S(2)}) collective-permute-start(f32[512,16]{0,1:T(8,128)} %reduce_sum.173), channel_id=1, source_target_pairs={{0,1},{1,0},{2,3},{3,2},{4,5},{5,4},{6,7},{7,6},{8,9},{9,8},{10,11... | collective-permute-start | bytes 98312 | tf_op jit(solution)/shard_map/ppermute | solution.py:37
  482.4 7.6 collective-permute-start.41
  487.1 6.1 collective-permute-start.46
  489.5 4.1 collective-permute-start.44
  490.8 3.9 collective-permute-start.42
  506.2 254.0 %all-reduce.2.cloned.1.call-start = ((), (), s32[]{:S(2)}) async-start(), calls=%async_computation.4 | async-start | bytes 3145728 | tf_op jit(solution)/shard_map/psum | solution.py:323
  532.3 3.1 collective-permute-start.39
  535.3 4.9 collective-permute-start.38
  535.5 14.5 %collective-permute-start.40 = (bf16[128,2048]{1,0:T(8,128)(2,1)S(1)}, bf16[128,2048]{1,0:T(8,128)(2,1)}, u32[]{:S(2)}, u32[]{:S(2)}) collective-permute-start(bf16[128,2048]{1,0:T(8,128)(2,1)S(1)} %add_convert_fusion.3), channel_id=1, source_target_pairs={{0,2},{2,0},{1,3},{3,1},{4,6},{6,4},{5,7},{7,5},{8,10},{10,8},{9,1... | collective-permute-start | bytes 1572872 | tf_op jit(solution)/shard_map/ppermute | solution.py:41
  (113 other events, 887.5 us)
Sparse Core Ops, SparseCore 0:
  506.3 162.2 all-gather.2
  672.7 87.4 all-reduce.1
